TPU v7x, 32 devices: a whole 2x2x4 slice. The times are simulated.
32 devices in a mesh: tm: 4 (over y, core), space: 8 (over z, x).
Axes of the slice: x: 2, y: 2, z: 4, core: 2. Of those that a mesh axis runs over, the one named last changes fastest.
Arguments:
- latent: bfloat16 [32, 32, 64, 256], P('tm', 'space'), may hold values from -6 to 6
- spatial_weight: bfloat16 [3, 3, 256, 256], replicated, may hold values from -0.125 to 0.125
- spatial_bias: float32 [256], replicated, may hold values from -3 to 3
- temporal_weight: bfloat16 [3, 256, 256], replicated, may hold values from -0.21875 to 0.21875
- temporal_bias: float32 [256], replicated, may hold values from -3 to 3
Outputs:
- upsampled: bfloat16 [32, 64, 128, 256], P(('tm', 'space'))
All inputs are finite; a program needn't handle non-finite values.
Results may differ from a plain program's by a relative error of at most 0.0032.
Values may be sent and summed in bfloat16 or wider, within the bound.
No kernel may reach another device: no remote copies, remote signals or barrier semaphores. Data moves between devices by JAX's collectives and lax.ppermute only.
A program may use at most 128 MiB of HBM per device.

v0:
```python
import jax
import jax.numpy as jnp
from jax import lax
from jax.sharding import PartitionSpec as P


def padded(cells, sides, width):
    for axis, dim in sides:
        count = lax.axis_size(axis)
        ends = count - 1
        head = lax.slice_in_dim(cells, 0, width, axis=dim)
        tail = lax.slice_in_dim(cells, cells.shape[dim] - width, cells.shape[dim], axis=dim)
        cells = jnp.concatenate(
            [
                lax.ppermute(tail, axis, [(i, (i + 1) % count) for i in range(ends)]),
                cells,
                lax.ppermute(head, axis, [((i + 1) % count, i) for i in range(ends)]),
            ],
            axis=dim,
        )
    return cells


def from_behind(block, axis, distance):
    devices = range(lax.axis_size(axis))
    route = [(i - distance, i) for i in devices if i - distance in devices]
    return lax.ppermute(block, axis, route)


def temporal_mix(earlier, hidden, latent, temporal_weight, temporal_bias):
    count, rows, cols, chans = hidden.shape
    joined = jnp.concatenate([earlier, hidden], axis=0)
    total = jnp.zeros((count * rows * cols, chans), jnp.float32)
    for k in range(3):
        piece = joined[k : k + count].reshape(count * rows * cols, chans)
        total = total + jnp.dot(piece, temporal_weight[k], preferred_element_type=jnp.float32)
    own = latent.reshape(count * rows * cols, chans).astype(jnp.float32)
    return (own + total + temporal_bias).astype(jnp.bfloat16).reshape(count, rows, cols, chans)


def body(latent, spatial_weight, spatial_bias, temporal_weight, temporal_bias):
    frames, rows, cols, chans = latent.shape
    bordered = padded(latent, (("space", 1),), 1)
    bordered = jnp.pad(bordered, ((0, 0), (0, 0), (1, 1), (0, 0)))
    total = jnp.zeros((frames * rows * cols, chans), jnp.float32)
    for a in range(3):
        for b in range(3):
            tile = bordered[:, a : a + rows, b : b + cols, :].reshape(frames * rows * cols, chans)
            total = total + jnp.dot(tile, spatial_weight[a, b], preferred_element_type=jnp.float32)
    hidden = (
        jax.nn.silu(total + spatial_bias).astype(jnp.bfloat16).reshape(frames, rows, cols, chans)
    )
    earlier = from_behind(hidden[frames - 2 :], "tm", 1)
    local_mixed = temporal_mix(earlier, hidden, latent, temporal_weight, temporal_bias)
    mixed = lax.all_to_all(local_mixed, "space", split_axis=0, concat_axis=1, tiled=True)
    count, height, width, depth = mixed.shape
    grown = jnp.broadcast_to(mixed[:, :, None, :, None, :], (count, height, 2, width, 2, depth))
    return grown.reshape(count, 2 * height, 2 * width, depth)


def solution(mesh):
    in_specs = (P("tm", "space", None, None), P(), P(), P(), P())
    out_specs = P(("tm", "space"), None, None, None)
    return jax.shard_map(body, mesh=mesh, in_specs=in_specs, out_specs=out_specs, check_vma=False)
```

profile of v0, /device:TPU:1, one launch (start us, length us, event | category | flops | bytes accessed | tf_op | source)
XLA Modules:
  0.0 77.4 jit_solution(11071638202679942732)
XLA Ops:
  0.0 1.1 %fusion.40 = (bf16[8,1,64,256]{3,2,1,0:T(8,128)(2,1)S(1)}, bf16[8,1,64,256]{3,2,1,0:T(8,128)(2,1)S(1)}) fusion(bf16[8,4,64,256]{3,2,1,0:T(8,128)(2,1)} %param.5), kind=kLoop, calls=%fused_computation.57 | loop fusion | bytes 1048576 | tf_op jit(solution)/shard_map/slice | solution.py:12
  1.1 4.0 %collective-permute-start = (bf16[8,1,64,256]{3,2,1,0:T(8,128)(2,1)S(1)}, bf16[8,1,64,256]{3,2,1,0:T(8,128)(2,1)S(1)}, u32[]{:S(2)}, u32[]{:S(2)}) collective-permute-start(bf16[8,1,64,256]{3,2,1,0:T(8,128)(2,1)S(1)} %get-tuple-element.15), channel_id=1, source_target_pairs={{0,1},{1,2},{2,3},{3,4},{4,5},{5,6},{6,7},{8,9},{9,10},{10,11},{11... | collective-permute-start | bytes 786440 | tf_op jit(solution)/shard_map/ppermute | solution.py:15
  5.0 1.3 %collective-permute-start.1 = (bf16[8,1,64,256]{3,2,1,0:T(8,128)(2,1)S(1)}, bf16[8,1,64,256]{3,2,1,0:T(8,128)(2,1)S(1)}, u32[]{:S(2)}, u32[]{:S(2)}) collective-permute-start(bf16[8,1,64,256]{3,2,1,0:T(8,128)(2,1)S(1)} %get-tuple-element.16), channel_id=1, source_target_pairs={{1,0},{2,1},{3,2},{4,3},{5,4},{6,5},{7,6},{9,8},{10,9},{11,10},{12... | collective-permute-start | bytes 786440 | tf_op jit(solution)/shard_map/ppermute | solution.py:17
  6.3 3.5 %collective-permute-done = bf16[8,1,64,256]{3,2,1,0:T(8,128)(2,1)S(1)} collective-permute-done((bf16[8,1,64,256]{3,2,1,0:T(8,128)(2,1)S(1)}, bf16[8,1,64,256]{3,2,1,0:T(8,128)(2,1)S(1)}, u32[]{:S(2)}, u32[]{:S(2)}) %collective-permute-start) | collective-permute-done | bytes 262176 | tf_op jit(solution)/shard_map/ppermute | solution.py:15
  9.9 3.9 %collective-permute-done.1 = bf16[8,1,64,256]{3,2,1,0:T(8,128)(2,1)S(1)} collective-permute-done((bf16[8,1,64,256]{3,2,1,0:T(8,128)(2,1)S(1)}, bf16[8,1,64,256]{3,2,1,0:T(8,128)(2,1)S(1)}, u32[]{:S(2)}, u32[]{:S(2)}) %collective-permute-start.1) | collective-permute-done | bytes 262176 | tf_op jit(solution)/shard_map/ppermute | solution.py:17
  13.8 2.1 %fusion.10 = bf16[8,6,66,256]{3,2,1,0:T(8,128)(2,1)S(1)} fusion(bf16[8,1,64,256]{3,2,1,0:T(8,128)(2,1)S(1)} %collective-permute-done.1, bf16[8,4,64,256]{3,2,1,0:T(8,128)(2,1)} %param.5, bf16[8,1,64,256]{3,2,1,0:T(8,128)(2,1)S(1)} %collective-permute-done), kind=kLoop, calls=%fused_computation.22 | loop fusion | flops 9732096 | bytes 3194880 | tf_op jit(solution)/shard_map/concatenate | solution.py:13
  16.0 1.2 %fusion.39 = (bf16[8,4,64,256]{3,2,1,0:T(8,128)(2,1)S(1)}, bf16[8,4,64,256]{3,2,1,0:T(8,128)(2,1)S(1)}, bf16[8,4,64,256]{3,2,1,0:T(8,128)(2,1)S(1)}, bf16[8,4,64...) fusion(bf16[8,6,66,256]{3,2,1,0:T(8,128)(2,1)S(1)} %fusion.10), kind=kLoop, calls=%fused_computation.56 | loop fusion | bytes 12582912 | tf_op jit(solution)/shard_map/slice | solution.py:48
  17.2 0.4 fusion.25
  18.1 0.8 %copy-done = bf16[8,4,64,256]{3,2,1,0:T(8,128)(2,1)S(1)} copy-done((bf16[8,4,64,256]{3,2,1,0:T(8,128)(2,1)S(1)}, bf16[8,4,64,256]{3,2,1,0:T(8,128)(2,1)}, u32[]{:S(2)}) %copy-start) | copy-done | bytes 1048600
  19.0 0.4 convolution_add_fusion.8
  19.5 0.4 convolution_add_fusion.7
  19.9 0.4 convolution_add_fusion.6
  20.4 0.4 convolution_add_fusion.5
  20.8 0.4 convolution_add_fusion.4
  21.3 0.4 convolution_add_fusion.3
  21.9 0.8 %multiply_convert_fusion = bf16[2048,256]{1,0:T(8,128)(2,1)S(1)} fusion(f32[2048,256]{1,0:T(8,128)S(1)} %fusion.16, f32[2048,256]{1,0:T(8,128)S(1)} %convolution_add_fusion.3, bf16[2048,256]{1,0:T(8,128)(2,1)S(1)} %bitcast.77, f32[256]{0:T(256)S(1)} %copy-done.4, bf16[3,3,256,256]{3,2,1,0:T(8,128)(2,1)S(1)} %copy-done.1), kind=kOutput, calls=%fused_computation.17 | convolution fusion | flops 272629760 | bytes 6423552 | tf_op jit(solution)/shard_map/dot_general | solution.py:49
  22.8 6.5 %collective-permute-start.2 = (bf16[2,4,64,256]{3,2,1,0:T(8,128)(2,1)S(1)}, bf16[2,4,64,256]{3,2,1,0:T(8,128)(2,1)S(1)}, u32[]{:S(2)}, u32[]{:S(2)}) collective-permute-start(bf16[2,4,64,256]{3,2,1,0:T(8,128)(2,1)S(1)} %bitcast.78), channel_id=1, source_target_pairs={{0,8},{8,16},{16,24},{1,9},{9,17},{17,25},{2,10},{10,18},{18,26},{... | collective-permute-start | bytes 786440 | tf_op jit(solution)/shard_map/ppermute | solution.py:27
  29.3 3.3 %collective-permute-done.2 = bf16[2,4,64,256]{3,2,1,0:T(8,128)(2,1)S(1)} collective-permute-done((bf16[2,4,64,256]{3,2,1,0:T(8,128)(2,1)S(1)}, bf16[2,4,64,256]{3,2,1,0:T(8,128)(2,1)S(1)}, u32[]{:S(2)}, u32[]{:S(2)}) %collective-permute-start.2) | collective-permute-done | bytes 262176 | tf_op jit(solution)/shard_map/ppermute | solution.py:27
  32.8 0.4 fusion.13
  33.2 0.5 convolution_add_fusion.1
  33.9 0.5 fusion.5
  34.4 29.8 %all_to_all.4 = bf16[8,4,64,256]{3,2,1,0:T(8,128)(2,1)S(1)} all-to-all(bf16[8,4,64,256]{3,2,1,0:T(8,128)(2,1)S(1)} %bitcast.76), channel_id=1, replica_groups=mesh['tm'=4,'space'=8] {'space'}, dimensions={0} | all-to-all | bytes 2097152 | tf_op jit(solution)/shard_map/all_to_all | solution.py:55
  64.2 6.0 %broadcast_in_dim.13 = bf16[32,2,64,2,256]{4,3,2,1,0:T(2,128)(2,1)} broadcast(bf16[32,64,256]{2,1,0:T(8,128)(2,1)S(1)} %bitcast.69), dimensions={0,2,4} | broadcast | bytes 5242880 | tf_op jit(solution)/shard_map/broadcast_in_dim | solution.py:57
  70.2 7.2 %broadcast_in_dim.14 = bf16[1,64,128,256]{3,2,1,0:T(8,128)(2,1)} reshape(bf16[32,2,64,2,256]{4,3,2,1,0:T(2,128)(2,1)} %broadcast_in_dim.13) | data formatting | bytes 8388608 | tf_op jit(solution)/shard_map/broadcast_in_dim | solution.py:57
  (13 shorter events, 1.2 us)
Async XLA Ops:
  1.1 8.8 %collective-permute-start = (bf16[8,1,64,256]{3,2,1,0:T(8,128)(2,1)S(1)}, bf16[8,1,64,256]{3,2,1,0:T(8,128)(2,1)S(1)}, u32[]{:S(2)}, u32[]{:S(2)}) collective-permute-start(bf16[8,1,64,256]{3,2,1,0:T(8,128)(2,1)S(1)} %get-tuple-element.15), channel_id=1, source_target_pairs={{0,1},{1,2},{2,3},{3,4},{4,5},{5,6},{6,7},{8,9},{9,10},{10,11},{11... | collective-permute-start | bytes 786440 | tf_op jit(solution)/shard_map/ppermute | solution.py:15
  5.0 8.8 %collective-permute-start.1 = (bf16[8,1,64,256]{3,2,1,0:T(8,128)(2,1)S(1)}, bf16[8,1,64,256]{3,2,1,0:T(8,128)(2,1)S(1)}, u32[]{:S(2)}, u32[]{:S(2)}) collective-permute-start(bf16[8,1,64,256]{3,2,1,0:T(8,128)(2,1)S(1)} %get-tuple-element.16), channel_id=1, source_target_pairs={{1,0},{2,1},{3,2},{4,3},{5,4},{6,5},{7,6},{9,8},{10,9},{11,10},{12... | collective-permute-start | bytes 786440 | tf_op jit(solution)/shard_map/ppermute | solution.py:17
  15.9 1.3 %copy-start.1 = (bf16[3,3,256,256]{3,2,1,0:T(8,128)(2,1)S(1)}, bf16[3,3,256,256]{3,2,1,0:T(8,128)(2,1)}, u32[]{:S(2)}) copy-start(bf16[3,3,256,256]{3,2,1,0:T(8,128)(2,1)} %param.6) | copy-start | bytes 3538948
  17.6 1.2 %copy-start = (bf16[8,4,64,256]{3,2,1,0:T(8,128)(2,1)S(1)}, bf16[8,4,64,256]{3,2,1,0:T(8,128)(2,1)}, u32[]{:S(2)}) copy-start(bf16[8,4,64,256]{3,2,1,0:T(8,128)(2,1)} %param.5) | copy-start | bytes 3145732
  21.2 0.7 copy-start.4
  22.8 10.0 %copy-start.2 = (bf16[3,256,256]{2,1,0:T(8,128)(2,1)S(1)}, bf16[3,256,256]{2,1,0:T(8,128)(2,1)}, u32[]{:S(2)}) copy-start(bf16[3,256,256]{2,1,0:T(8,128)(2,1)} %param.8) | copy-start | bytes 1179652
  22.8 9.8 %collective-permute-start.2 = (bf16[2,4,64,256]{3,2,1,0:T(8,128)(2,1)S(1)}, bf16[2,4,64,256]{3,2,1,0:T(8,128)(2,1)S(1)}, u32[]{:S(2)}, u32[]{:S(2)}) collective-permute-start(bf16[2,4,64,256]{3,2,1,0:T(8,128)(2,1)S(1)} %bitcast.78), channel_id=1, source_target_pairs={{0,8},{8,16},{16,24},{1,9},{9,17},{17,25},{2,10},{10,18},{18,26},{... | collective-permute-start | bytes 786440 | tf_op jit(solution)/shard_map/ppermute | solution.py:27
  33.2 0.7 copy-start.3
where the time goes:
time: 77.9 us; the launch traced here: 77.4 us
  blocking collectives  29.8 us (38%)
  local copies, waits for them, and re-layouts  16.8 us (22%)
  starting transfers between devices  11.8 us (15%)
  waiting for transfers between devices  10.7 us (14%)
  matrix products  5.67 us (7%)
  other arithmetic  2.43 us (3%)
    all_to_all x1, blocking collectives, body(): lax.all_to_all(local_mixed, 'space', split_axis=0, concat_axis=1, tiled=T...  29.8 us
    broadcast_in_dim x2, local copies, waits for them, and re-layouts, body(): jnp.broadcast_to(mixed[:, :, None, :, None, :], (count, height, 2, width,...  13.2 us
    ppermute x1, starting transfers between devices, from_behind(): return lax.ppermute(block, axis, route)  6.52 us
    dot_general x9, matrix products, body(): jnp.dot(tile, spatial_weight[a, b], preferred_element_type=jnp.float32)  4.29 us
    ppermute x1, starting transfers between devices, padded(): lax.ppermute(tail, axis, [(i, (i + 1) % count) for i in range(ends)])  3.96 us
    ppermute x1, waiting for transfers between devices, padded(): lax.ppermute(head, axis, [((i + 1) % count, i) for i in range(ends)])  3.94 us
    ppermute x1, waiting for transfers between devices, padded(): lax.ppermute(tail, axis, [(i, (i + 1) % count) for i in range(ends)])  3.51 us
    ppermute x1, waiting for transfers between devices, from_behind(): return lax.ppermute(block, axis, route)  3.29 us
  transfers between devices with their start and end apart: 3, of which 3 were waited for; matrix products, arithmetic and copies ran while one was open for 0% of the time, Pallas kernels for 0%

commit v1 on v0

--- a/solution.py
+++ b/solution.py
@@ -2,6 +2,7 @@
 import jax.numpy as jnp
 from jax import lax
 from jax.sharding import PartitionSpec as P
+from jax.lax import all_to_all, axis_size
 
 
 def padded(cells, sides, width):
@@ -52,7 +53,19 @@
     )
     earlier = from_behind(hidden[frames - 2 :], "tm", 1)
     local_mixed = temporal_mix(earlier, hidden, latent, temporal_weight, temporal_bias)
-    mixed = lax.all_to_all(local_mixed, "space", split_axis=0, concat_axis=1, tiled=True)
+
+    def advance_bars(sheet, d0, axis_no):
+        return jnp.concatenate(
+            all_to_all(
+                jnp.stack(jnp.split(sheet, axis_size("space"), d0), axis=0),
+                axis_name="space",
+                split_axis=0,
+                concat_axis=0,
+            ),
+            axis_no,
+        )
+
+    mixed = advance_bars(local_mixed, 0, 1)
     count, height, width, depth = mixed.shape
     grown = jnp.broadcast_to(mixed[:, :, None, :, None, :], (count, height, 2, width, 2, depth))
     return grown.reshape(count, 2 * height, 2 * width, depth)

time: 77.9 us -> 78.2 us (level)
  no operation moved by 1% of the time
where the time goes in v1:
time: 78.2 us; the launch traced here: 77.7 us
  blocking collectives  29.8 us (38%)
  local copies, waits for them, and re-layouts  17 us (22%)
  starting transfers between devices  11.8 us (15%)
  waiting for transfers between devices  10.7 us (14%)
  matrix products  5.74 us (7%)
  other arithmetic  2.43 us (3%)
    all_to_all x1, blocking collectives, advance_bars(): all_to_all(jnp.stack(jnp.split(sheet, axis_size('space'), d0), axis=0), a...  29.8 us
    broadcast_in_dim x2, local copies, waits for them, and re-layouts, body(): jnp.broadcast_to(mixed[:, :, None, :, None, :], (count, height, 2, width,...  13.2 us
    ppermute x1, starting transfers between devices, from_behind(): return lax.ppermute(block, axis, route)  6.52 us
    dot_general x9, matrix products, body(): jnp.dot(tile, spatial_weight[a, b], preferred_element_type=jnp.float32)  4.32 us
    ppermute x1, starting transfers between devices, padded(): lax.ppermute(tail, axis, [(i, (i + 1) % count) for i in range(ends)])  3.96 us
    ppermute x1, waiting for transfers between devices, padded(): lax.ppermute(head, axis, [((i + 1) % count, i) for i in range(ends)])  3.94 us
    ppermute x1, waiting for transfers between devices, padded(): lax.ppermute(tail, axis, [(i, (i + 1) % count) for i in range(ends)])  3.51 us
    ppermute x1, waiting for transfers between devices, from_behind(): return lax.ppermute(block, axis, route)  3.29 us
  transfers between devices with their start and end apart: 3, of which 3 were waited for; matrix products, arithmetic and copies ran while one was open for 0% of the time, Pallas kernels for 0%

profile of v1, /device:TPU:1, one launch (start us, length us, event | category | flops | bytes accessed | tf_op | source)
XLA Modules:
  0.0 77.7 jit_solution(9905253987468928053)
XLA Ops:
  0.0 1.1 %fusion.41 = (bf16[8,1,64,256]{3,2,1,0:T(8,128)(2,1)S(1)}, bf16[8,1,64,256]{3,2,1,0:T(8,128)(2,1)S(1)}) fusion(bf16[8,4,64,256]{3,2,1,0:T(8,128)(2,1)} %param.5), kind=kLoop, calls=%fused_computation.66 | loop fusion | bytes 1048576 | tf_op jit(solution)/shard_map/slice | solution.py:13
  1.1 4.0 %collective-permute-start = (bf16[8,1,64,256]{3,2,1,0:T(8,128)(2,1)S(1)}, bf16[8,1,64,256]{3,2,1,0:T(8,128)(2,1)S(1)}, u32[]{:S(2)}, u32[]{:S(2)}) collective-permute-start(bf16[8,1,64,256]{3,2,1,0:T(8,128)(2,1)S(1)} %get-tuple-element.23), channel_id=1, source_target_pairs={{0,1},{1,2},{2,3},{3,4},{4,5},{5,6},{6,7},{8,9},{9,10},{10,11},{11... | collective-permute-start | bytes 786440 | tf_op jit(solution)/shard_map/ppermute | solution.py:16
  5.0 1.3 %collective-permute-start.1 = (bf16[8,1,64,256]{3,2,1,0:T(8,128)(2,1)S(1)}, bf16[8,1,64,256]{3,2,1,0:T(8,128)(2,1)S(1)}, u32[]{:S(2)}, u32[]{:S(2)}) collective-permute-start(bf16[8,1,64,256]{3,2,1,0:T(8,128)(2,1)S(1)} %get-tuple-element.24), channel_id=1, source_target_pairs={{1,0},{2,1},{3,2},{4,3},{5,4},{6,5},{7,6},{9,8},{10,9},{11,10},{12... | collective-permute-start | bytes 786440 | tf_op jit(solution)/shard_map/ppermute | solution.py:18
  6.3 3.5 %collective-permute-done = bf16[8,1,64,256]{3,2,1,0:T(8,128)(2,1)S(1)} collective-permute-done((bf16[8,1,64,256]{3,2,1,0:T(8,128)(2,1)S(1)}, bf16[8,1,64,256]{3,2,1,0:T(8,128)(2,1)S(1)}, u32[]{:S(2)}, u32[]{:S(2)}) %collective-permute-start) | collective-permute-done | bytes 262176 | tf_op jit(solution)/shard_map/ppermute | solution.py:16
  9.8 3.9 %collective-permute-done.1 = bf16[8,1,64,256]{3,2,1,0:T(8,128)(2,1)S(1)} collective-permute-done((bf16[8,1,64,256]{3,2,1,0:T(8,128)(2,1)S(1)}, bf16[8,1,64,256]{3,2,1,0:T(8,128)(2,1)S(1)}, u32[]{:S(2)}, u32[]{:S(2)}) %collective-permute-start.1) | collective-permute-done | bytes 262176 | tf_op jit(solution)/shard_map/ppermute | solution.py:18
  13.8 2.1 %fusion.10 = bf16[8,6,66,256]{3,2,1,0:T(8,128)(2,1)S(1)} fusion(bf16[8,1,64,256]{3,2,1,0:T(8,128)(2,1)S(1)} %collective-permute-done.1, bf16[8,4,64,256]{3,2,1,0:T(8,128)(2,1)} %param.5, bf16[8,1,64,256]{3,2,1,0:T(8,128)(2,1)S(1)} %collective-permute-done), kind=kLoop, calls=%fused_computation.22 | loop fusion | flops 9732096 | bytes 3194880 | tf_op jit(solution)/shard_map/concatenate | solution.py:14
  15.9 1.3 %fusion.39 = (bf16[8,4,64,256]{3,2,1,0:T(8,128)(2,1)S(1)}, bf16[8,4,64,256]{3,2,1,0:T(8,128)(2,1)S(1)}, bf16[8,4,64,256]{3,2,1,0:T(8,128)(2,1)S(1)}, bf16[8,4,64...) fusion(bf16[8,6,66,256]{3,2,1,0:T(8,128)(2,1)S(1)} %fusion.10), kind=kLoop, calls=%fused_computation.64 | loop fusion | bytes 12582912 | tf_op jit(solution)/shard_map/slice | solution.py:49
  17.3 0.4 fusion.25
  17.7 0.4 fusion.16
  18.2 0.8 %copy-done = bf16[8,4,64,256]{3,2,1,0:T(8,128)(2,1)S(1)} copy-done((bf16[8,4,64,256]{3,2,1,0:T(8,128)(2,1)S(1)}, bf16[8,4,64,256]{3,2,1,0:T(8,128)(2,1)}, u32[]{:S(2)}) %copy-start) | copy-done | bytes 1048600
  19.1 0.4 convolution_add_fusion.8
  19.5 0.4 convolution_add_fusion.7
  20.0 0.4 convolution_add_fusion.6
  20.4 0.5 convolution_add_fusion.5
  20.9 0.4 convolution_add_fusion.4
  21.3 0.4 convolution_add_fusion.3
  22.0 0.8 %multiply_convert_fusion = bf16[2048,256]{1,0:T(8,128)(2,1)S(1)} fusion(f32[2048,256]{1,0:T(8,128)S(1)} %fusion.16, f32[2048,256]{1,0:T(8,128)S(1)} %convolution_add_fusion.3, bf16[2048,256]{1,0:T(8,128)(2,1)S(1)} %bitcast.83, f32[256]{0:T(256)S(1)} %copy-done.4, bf16[3,3,256,256]{3,2,1,0:T(8,128)(2,1)S(1)} %copy-done.1), kind=kOutput, calls=%fused_computation.17 | convolution fusion | flops 272629760 | bytes 6423552 | tf_op jit(solution)/shard_map/dot_general | solution.py:50
  22.9 6.5 %collective-permute-start.2 = (bf16[2,4,64,256]{3,2,1,0:T(8,128)(2,1)S(1)}, bf16[2,4,64,256]{3,2,1,0:T(8,128)(2,1)S(1)}, u32[]{:S(2)}, u32[]{:S(2)}) collective-permute-start(bf16[2,4,64,256]{3,2,1,0:T(8,128)(2,1)S(1)} %bitcast.92), channel_id=1, source_target_pairs={{0,8},{8,16},{16,24},{1,9},{9,17},{17,25},{2,10},{10,18},{18,26},{... | collective-permute-start | bytes 786440 | tf_op jit(solution)/shard_map/ppermute | solution.py:28
  29.4 3.3 %collective-permute-done.2 = bf16[2,4,64,256]{3,2,1,0:T(8,128)(2,1)S(1)} collective-permute-done((bf16[2,4,64,256]{3,2,1,0:T(8,128)(2,1)S(1)}, bf16[2,4,64,256]{3,2,1,0:T(8,128)(2,1)S(1)}, u32[]{:S(2)}, u32[]{:S(2)}) %collective-permute-start.2) | collective-permute-done | bytes 262176 | tf_op jit(solution)/shard_map/ppermute | solution.py:28
  33.3 0.5 convolution_add_fusion.1
  34.0 0.5 fusion.5
  34.7 29.8 %all_to_all.5 = bf16[8,1,4,64,256]{4,3,2,1,0:T(8,128)(2,1)S(1)} all-to-all(bf16[8,1,4,64,256]{4,3,2,1,0:T(8,128)(2,1)S(1)} %constant_dynamic-update-slice_fusion), channel_id=1, replica_groups=mesh['tm'=4,'space'=8] {'space'}, dimensions={0} | all-to-all | bytes 2097152 | tf_op jit(solution)/shard_map/all_to_all | solution.py:59
  64.5 6.0 %broadcast_in_dim.12 = bf16[32,2,64,2,256]{4,3,2,1,0:T(2,128)(2,1)} broadcast(bf16[32,64,256]{2,1,0:T(8,128)(2,1)S(1)} %bitcast.76), dimensions={0,2,4} | broadcast | bytes 5242880 | tf_op jit(solution)/shard_map/broadcast_in_dim | solution.py:70
  70.5 7.2 %broadcast_in_dim.13 = bf16[1,64,128,256]{3,2,1,0:T(8,128)(2,1)} reshape(bf16[32,2,64,2,256]{4,3,2,1,0:T(2,128)(2,1)} %broadcast_in_dim.12) | data formatting | bytes 8388608 | tf_op jit(solution)/shard_map/broadcast_in_dim | solution.py:70
  (22 shorter events, 1.3 us)
Async XLA Ops:
  1.1 8.8 %collective-permute-start = (bf16[8,1,64,256]{3,2,1,0:T(8,128)(2,1)S(1)}, bf16[8,1,64,256]{3,2,1,0:T(8,128)(2,1)S(1)}, u32[]{:S(2)}, u32[]{:S(2)}) collective-permute-start(bf16[8,1,64,256]{3,2,1,0:T(8,128)(2,1)S(1)} %get-tuple-element.23), channel_id=1, source_target_pairs={{0,1},{1,2},{2,3},{3,4},{4,5},{5,6},{6,7},{8,9},{9,10},{10,11},{11... | collective-permute-start | bytes 786440 | tf_op jit(solution)/shard_map/ppermute | solution.py:16
  5.0 8.8 %collective-permute-start.1 = (bf16[8,1,64,256]{3,2,1,0:T(8,128)(2,1)S(1)}, bf16[8,1,64,256]{3,2,1,0:T(8,128)(2,1)S(1)}, u32[]{:S(2)}, u32[]{:S(2)}) collective-permute-start(bf16[8,1,64,256]{3,2,1,0:T(8,128)(2,1)S(1)} %get-tuple-element.24), channel_id=1, source_target_pairs={{1,0},{2,1},{3,2},{4,3},{5,4},{6,5},{7,6},{9,8},{10,9},{11,10},{12... | collective-permute-start | bytes 786440 | tf_op jit(solution)/shard_map/ppermute | solution.py:18
  15.9 1.3 %copy-start.1 = (bf16[3,3,256,256]{3,2,1,0:T(8,128)(2,1)S(1)}, bf16[3,3,256,256]{3,2,1,0:T(8,128)(2,1)}, u32[]{:S(2)}) copy-start(bf16[3,3,256,256]{3,2,1,0:T(8,128)(2,1)} %param.6) | copy-start | bytes 3538948
  17.7 1.2 %copy-start = (bf16[8,4,64,256]{3,2,1,0:T(8,128)(2,1)S(1)}, bf16[8,4,64,256]{3,2,1,0:T(8,128)(2,1)}, u32[]{:S(2)}) copy-start(bf16[8,4,64,256]{3,2,1,0:T(8,128)(2,1)} %param.5) | copy-start | bytes 3145732
  21.3 0.7 copy-start.4
  22.8 10.0 %copy-start.2 = (bf16[3,256,256]{2,1,0:T(8,128)(2,1)S(1)}, bf16[3,256,256]{2,1,0:T(8,128)(2,1)}, u32[]{:S(2)}) copy-start(bf16[3,256,256]{2,1,0:T(8,128)(2,1)} %param.8) | copy-start | bytes 1179652
  22.9 9.8 %collective-permute-start.2 = (bf16[2,4,64,256]{3,2,1,0:T(8,128)(2,1)S(1)}, bf16[2,4,64,256]{3,2,1,0:T(8,128)(2,1)S(1)}, u32[]{:S(2)}, u32[]{:S(2)}) collective-permute-start(bf16[2,4,64,256]{3,2,1,0:T(8,128)(2,1)S(1)} %bitcast.92), channel_id=1, source_target_pairs={{0,8},{8,16},{16,24},{1,9},{9,17},{17,25},{2,10},{10,18},{18,26},{... | collective-permute-start | bytes 786440 | tf_op jit(solution)/shard_map/ppermute | solution.py:28
  33.3 0.7 copy-start.3
